TPU v7x, 256 devices: a whole 4x4x8 slice. The times are simulated.
256 devices in a mesh: seq: 64 (over x, z_hi, y), heads: 4 (over z_lo, core).
Axes of the slice: x: 4, y: 4, z: 8 (z_hi: 4, z_lo: 2; z = z_hi * 2 + z_lo), core: 2. Of those that a mesh axis runs over, the one named last changes fastest.
Arguments:
- queries: bfloat16 [131072, 2048], P('seq', 'heads'), may hold values from -120 to 120
- keys: bfloat16 [512, 2048], P(None, 'heads'), may hold values from -4.2 to 4.2
- values: bfloat16 [512, 2048], P(None, 'heads'), may hold values from -6 to 6
- out_grad: bfloat16 [131072, 2048], P('seq', 'heads'), may hold values from -6 to 6
- key_proj: bfloat16 [2048, 2048], P(None, 'heads'), may hold values from -0.125 to 0.125
- value_proj: bfloat16 [2048, 2048], P(None, 'heads'), may hold values from -0.125 to 0.125
- global_in: bfloat16 [512, 2048], P('seq', 'heads'), may hold values from -6 to 6
- up_proj: bfloat16 [2048, 8192], P('heads', 'seq'), may hold values from -0.125 to 0.125
- down_proj: bfloat16 [8192, 2048], P('seq', 'heads'), may hold values from -0.0625 to 0.0625
Outputs:
- query_grad: bfloat16 [131072, 2048], P('seq', 'heads')
- global_grad: float32 [512, 2048], P('seq', 'heads')
All inputs are finite; a program needn't handle non-finite values.
Results may differ from a plain program's by a relative error of at most 0.014.
Values may be sent and summed in bfloat16 or wider, within the bound.
A program may use at most 128 MiB of HBM per device.

v0:
```python
import jax
import jax.numpy as jnp
from jax import lax
from jax.sharding import PartitionSpec as P

HD = 128


def slope_of(pre):
    return (
        0.5 * (1.0 + lax.erf(pre * 0.7071067811865476))
        + pre * jnp.exp(-0.5 * pre * pre) * 0.3989422804014327
    )


def project(key_sum, value_sum, key_proj, value_proj):
    first = jnp.einsum(
        "gc,dc->gd", key_sum.astype(jnp.bfloat16), key_proj, preferred_element_type=jnp.float32
    )
    second = jnp.einsum(
        "gc,dc->gd", value_sum.astype(jnp.bfloat16), value_proj, preferred_element_type=jnp.float32
    )
    return first + second


def local(queries, keys, values, out_grad, key_proj, value_proj, global_in, up_proj, down_proj):
    tok_rows, width = queries.shape
    glob_rows = keys.shape[0]
    local_heads = width // HD
    scale = HD ** (-0.5)
    block = min(512, tok_rows)
    blocks = tok_rows // block
    pre_part = jnp.dot(
        lax.all_gather(global_in, "seq", axis=0, tiled=True),
        up_proj,
        preferred_element_type=jnp.float32,
    )
    key_heads = keys.reshape(glob_rows, local_heads, HD)
    value_heads = values.reshape(glob_rows, local_heads, HD)
    query_blocks = queries.reshape(blocks, block, local_heads, HD)
    grad_blocks = out_grad.reshape(blocks, block, local_heads, HD)

    def attend(carry, pair):
        key_total, value_total = carry
        query_block, grad_block = pair
        scores = scale * jnp.einsum(
            "rhd,ghd->hrg", query_block, key_heads, preferred_element_type=jnp.float32
        )
        weights = jax.nn.softmax(scores, axis=-1)
        weight_grad = jnp.einsum(
            "rhd,ghd->hrg", grad_block, value_heads, preferred_element_type=jnp.float32
        )
        centre = jnp.sum(weights * weight_grad, axis=-1, keepdims=True)
        score_grad = (weights * (weight_grad - centre)).astype(jnp.bfloat16)
        weights_low = weights.astype(jnp.bfloat16)
        block_grad = (
            scale
            * jnp.einsum("hrg,ghd->rhd", score_grad, key_heads, preferred_element_type=jnp.float32)
        ).astype(jnp.bfloat16)
        key_total = key_total + jnp.einsum(
            "hrg,rhd->ghd", score_grad, query_block, preferred_element_type=jnp.float32
        )
        value_total = value_total + jnp.einsum(
            "hrg,rhd->ghd", weights_low, grad_block, preferred_element_type=jnp.float32
        )
        return ((key_total, value_total), block_grad)

    empty = jnp.zeros((glob_rows, local_heads, HD), jnp.float32)
    (key_total, value_total), block_grads = lax.scan(
        attend, (empty, empty), (query_blocks, grad_blocks)
    )
    query_grad = block_grads.reshape(tok_rows, width)
    key_total = scale * key_total.reshape(glob_rows, width)
    value_total = value_total.reshape(glob_rows, width)
    key_sum, value_sum = lax.psum((key_total, value_total), "seq")
    state_share = lax.psum_scatter(
        project(key_sum, value_sum, key_proj, value_proj).astype(jnp.bfloat16),
        "heads",
        scatter_dimension=1,
        tiled=True,
    ).astype(jnp.float32)
    state_low = state_share.astype(jnp.bfloat16)
    share_rows = glob_rows // lax.axis_size("seq")
    own_state = lax.dynamic_slice_in_dim(
        state_share, lax.axis_index("seq") * share_rows, share_rows, 0
    )
    back_part = jnp.einsum("gc,fc->gf", state_low, down_proj, preferred_element_type=jnp.float32)
    pre_total, back_total = (
        lax.psum(pre_part.astype(jnp.bfloat16), "heads").astype(jnp.float32),
        lax.psum(back_part.astype(jnp.bfloat16), "heads").astype(jnp.float32),
    )
    gated = (slope_of(pre_total) * back_total).astype(jnp.bfloat16)
    input_part = jnp.einsum("gf,cf->gc", gated, up_proj, preferred_element_type=jnp.float32)
    global_grad = own_state + lax.psum_scatter(input_part, "seq", scatter_dimension=0, tiled=True)
    return (query_grad, global_grad)


def solution(mesh):
    placed = (
        P("seq", "heads"),
        P(None, "heads"),
        P(None, "heads"),
        P("seq", "heads"),
        P(None, "heads"),
        P(None, "heads"),
        P("seq", "heads"),
        P("heads", "seq"),
        P("seq", "heads"),
    )
    return jax.shard_map(
        local,
        mesh=mesh,
        in_specs=placed,
        out_specs=(P("seq", "heads"), P("seq", "heads")),
        check_vma=False,
    )
```

profile of v0, /device:TPU:0, one launch (start us, length us, event | category | flops | bytes accessed | tf_op | source)
XLA Modules:
  0.0 1139.3 jit_solution(193295031529866412)
XLA Ops:
  7.2 0.0 reduce-scatter.3.cloned.1.call-start
  7.3 1.4 copy.22
  8.6 0.3 copy.25
  8.9 1.3 copy.23
  10.2 1.0 copy.27
  11.2 4.0 reshape.28
  15.2 4.0 reshape.30
  19.2 83.3 %while.15 = (s32[]{:T(128)}, f32[512,4,128]{0,2,1:T(8,128)}, f32[512,4,128]{0,2,1:T(8,128)}, bf16[4,512,4,128]{3,2,1,0:T(4,128)(2,1)}, bf16[4,512,4,128]{3,2,1,0...) while((s32[]{:T(128)}, f32[512,4,128]{0,2,1:T(8,128)}, ...), condition=%wide.region_4.5_spmd.clone, body=%wide.region_0.4_spmd.clone.sunk | while | flops 1360528384 | bytes 93372648 | solution.py:69
  19.2 2.4 constant_dynamic-slice_fusion.3
  21.5 0.7 fusion.81
  22.3 3.2 fusion.82
  25.5 6.4 fusion.84
  31.8 3.4 multiply_reduce_fusion.3
  35.2 0.4 copy-done.1
  35.6 1.2 multiply_convert_fusion.2
  36.8 0.0 copy-done.3
  36.8 0.9 fusion.83
  37.7 0.9 fusion.85
  38.6 1.2 copy_dynamic-update-slice_fusion.2
  39.9 2.4 constant_dynamic-slice_fusion.3
  42.2 0.7 fusion.81
  43.0 3.2 fusion.82
  46.1 6.6 fusion.84
  52.7 3.4 multiply_reduce_fusion.3
  56.1 0.4 copy-done.1
  56.5 1.2 multiply_convert_fusion.2
  57.7 0.9 fusion.83
  58.6 0.9 fusion.85
  59.5 1.2 copy_dynamic-update-slice_fusion.2
  60.7 2.4 constant_dynamic-slice_fusion.3
  63.1 0.7 fusion.81
  63.8 3.2 fusion.82
  67.0 6.6 fusion.84
  73.6 3.4 multiply_reduce_fusion.3
  77.0 0.4 copy-done.1
  77.3 1.2 multiply_convert_fusion.2
  78.6 0.9 fusion.83
  79.5 0.9 fusion.85
  80.4 1.2 copy_dynamic-update-slice_fusion.2
  81.6 2.4 constant_dynamic-slice_fusion.3
  84.0 0.7 fusion.81
  84.7 3.2 fusion.82
  87.9 6.6 fusion.84
  94.4 3.4 multiply_reduce_fusion.3
  97.8 0.4 copy-done.1
  98.2 1.2 multiply_convert_fusion.2
  99.4 0.9 fusion.83
  100.3 0.9 fusion.85
  101.3 1.2 copy_dynamic-update-slice_fusion.2
  102.5 2.3 broadcast_multiply_fusion
  104.8 403.6 %all-reduce.6 = (bf16[512,512]{0,1:T(8,128)(2,1)S(1)}, bf16[512,512]{0,1:T(8,128)(2,1)S(1)}) all-reduce(f32[512,512]{0,1:T(8,128)} %bitcast.69, f32[512,512]{0,1:T(8,128)} %bitcast.74), channel_id=1, replica_groups=mesh['seq'=64,'heads'=4] {'seq'}, use_global_device_ids=true, to_apply=%region_5.6 | all-reduce | flops 524288 | bytes 3145728 | tf_op jit(solution)/shard_map/psum | solution.py:75
  508.5 1.3 fusion.47
  509.8 0.3 copy-done.5
  510.0 2.6 add_convert_fusion
  512.7 0.0 all-reduce.5.cloned.1.call-start
  512.8 187.2 %all_gather.3 = bf16[512,512]{1,0:T(8,128)(2,1)S(1)} all-gather(bf16[8,512]{1,0:T(8,128)(2,1)S(1)} %copy-done.8), channel_id=1, replica_groups=mesh['seq'=64,'heads'=4] {'seq'}, dimensions={0}, use_global_device_ids=true | all-gather | bytes 532480 | tf_op jit(solution)/shard_map/all_gather | solution.py:34
  699.9 0.9 convolution_convert_fusion.1
  700.8 2.0 convolution_convert_fusion
  702.9 0.0 reduce-scatter.5.cloned.1.call-start
  702.9 38.1 %all-reduce.5.cloned.1.call-done = (bf16[512,128]{1,0:T(8,128)(2,1)}, bf16[512,128]{1,0:T(8,128)(2,1)}) async-done(((bf16[512,128]{1,0:T(8,128)(2,1)}, bf16[512,128]{1,0:T(8,128)(2,1)}), (bf16[512,128]{1,0:T(8,128)(2,1)}, bf16[512,128]{1,0:T(8,128)(2,1)})) %all-reduce.5.cloned.1.call-update) | async-done | bytes 262160 | tf_op jit(solution)/shard_map/psum | solution.py:90
  741.1 2.3 fusion.34
  743.3 3.3 copy.49
  746.6 384.8 %reduce-scatter.5.cloned.1.call-done = f32[8,512]{1,0:T(8,128)} async-done(((f32[512,512]{1,0:T(8,128)}), f32[8,512]{1,0:T(8,128)}) %reduce-scatter.5.cloned.1.call-update) | async-done | bytes 16400 | tf_op jit(solution)/shard_map/reduce_scatter | solution.py:94
  1131.4 1.3 convert_add_fusion
  (43 shorter events, 0.2 us)
Async XLA Ops:
  7.2 501.3 %copy-start = (bf16[2048,512]{1,0:T(8,128)(2,1)S(1)}, bf16[2048,512]{1,0:T(8,128)(2,1)}, u32[]{:S(2)}) copy-start(bf16[2048,512]{1,0:T(8,128)(2,1)} %param.15) | copy-start | bytes 6291460
  7.2 693.7 %reduce-scatter.3.cloned.1.call-start = ((), (), s32[]{:S(2)}) async-start(), calls=%async_computation.2 | async-start | bytes 2621440 | tf_op jit(solution)/shard_map/reduce_scatter | solution.py:76
  22.3 3.2 copy-start.2
  31.8 3.7 copy-start.1
  35.6 1.2 copy-start.3
  37.7 2.2 copy-start.4
  42.9 3.2 copy-start.2
  52.7 3.7 copy-start.1
  56.5 1.2 copy-start.3
  58.6 2.1 copy-start.4
  63.8 3.2 copy-start.2
  73.6 3.7 copy-start.1
  77.3 1.2 copy-start.3
  79.5 2.1 copy-start.4
  84.7 3.2 copy-start.2
  94.4 3.7 copy-start.1
  98.2 1.2 copy-start.3
  100.3 2.2 copy-start.4
  508.4 1.6 copy-start.5
  510.0 2.7 copy-start.8
  510.0 189.9 %copy-start.6 = (bf16[512,128]{1,0:T(8,128)(2,1)S(1)}, bf16[512,128]{1,0:T(8,128)(2,1)}, u32[]{:S(2)}) copy-start(bf16[512,128]{1,0:T(8,128)(2,1)} %param.18) | copy-start | bytes 393220
  510.0 190.8 %copy-start.7 = (bf16[128,512]{1,0:T(8,128)(2,1)S(1)}, bf16[128,512]{1,0:T(8,128)(2,1)}, u32[]{:S(2)}) copy-start(bf16[128,512]{1,0:T(8,128)(2,1)} %param.19) | copy-start | bytes 393220
  512.7 228.4 %all-reduce.5.cloned.1.call-start = ((), (), s32[]{:S(2)}) async-start(), calls=%async_computation.4 | async-start | bytes 524288 | tf_op jit(solution)/shard_map/psum | solution.py:90
  702.9 428.5 %reduce-scatter.5.cloned.1.call-start = ((), (), s32[]{:S(2)}) async-start(), calls=%async_computation.3 | async-start | bytes 1064960 | tf_op jit(solution)/shard_map/reduce_scatter | solution.py:94
Sparse Core Ops, SparseCore 0:
  512.8 27.8 reduce-scatter.2
  703.0 38.0 all-reduce.4
  743.6 387.8 reduce-scatter.4
where the time goes:
time: 1140 us
  blocking collectives  591 us (52%)
  waiting for transfers between devices  423 us (37%)
  matrix products  58.8 us (5%)
  local copies, waits for them, and re-layouts  31.5 us (3%)
  other arithmetic  21.1 us (2%)
  between operations  13.8 us (1%)
    psum x1, blocking collectives, local(): key_sum, value_sum = lax.psum((key_total, value_total), 'seq')  404 us
    reduce_scatter x1, waiting for transfers between devices, local(): lax.psum_scatter(input_part, 'seq', scatter_dimension=0, tiled=True)  385 us
    all_gather x1, blocking collectives, local(): lax.all_gather(global_in, 'seq', axis=0, tiled=True)  187 us
    psum x1, waiting for transfers between devices, local(): lax.psum(back_part.astype(jnp.bfloat16), 'heads').astype(jnp.float32)  38.1 us
    dot_general x4, matrix products, attend(): jnp.einsum('hrg,rhd->ghd', weights_low, grad_block, preferred_element_typ...  26.1 us
  transfers between devices with their start and end apart: 3, of which 2 were waited for; matrix products, arithmetic and copies ran while one was open for 0% of the time, Pallas kernels for 0%

commit v1 on v0

--- a/solution.py
+++ b/solution.py
@@ -4,6 +4,13 @@
 from jax.sharding import PartitionSpec as P
 
 HD = 128
+
+
+def gather_over(array, axis, along):
+    size = lax.axis_size(axis)
+    tiles = jnp.stack([array for _ in range(size)])
+    tiles = lax.all_to_all(tiles, axis, split_axis=0, concat_axis=0)
+    return jnp.concatenate(tiles, axis=along)
 
 
 def slope_of(pre):
@@ -31,9 +38,7 @@
     block = min(512, tok_rows)
     blocks = tok_rows // block
     pre_part = jnp.dot(
-        lax.all_gather(global_in, "seq", axis=0, tiled=True),
-        up_proj,
-        preferred_element_type=jnp.float32,
+        gather_over(global_in, "seq", 0), up_proj, preferred_element_type=jnp.float32
     )
     key_heads = keys.reshape(glob_rows, local_heads, HD)
     value_heads = values.reshape(glob_rows, local_heads, HD)

time: 1140 us -> 989 us (0.87)
  blocking collectives: 591 us -> 423 us
  waiting for transfers between devices: 423 us -> 440 us
    all_gather x1 -> x0, blocking collectives: 187 us -> none  [local(): lax.all_gather(global_in, 'seq', axis=0, tiled=True)]
    all_to_all x0 -> x1, blocking collectives: none -> 19.3 us  [gather_over(): tiles = lax.all_to_all(tiles, axis, split_axis=0, concat_axis=0)]
    reduce_scatter x1, waiting for transfers between devices: 0.01 us -> 11.9 us  [local(): lax.psum_scatter(project(key_sum, value_sum, key_proj, value_proj).astype...]
  transfers between devices with their start and end apart: 3 -> 3, of which waited for: 2 -> 3; matrix products, arithmetic and copies ran while one was open for 0% -> 0% of each run, Pallas kernels for 0% -> 0%
where the time goes in v1:
time: 989 us; the launch traced here: 988 us
  waiting for transfers between devices  440 us (44%)
  blocking collectives  423 us (43%)
  matrix products  58.8 us (6%)
  local copies, waits for them, and re-layouts  31.5 us (3%)
  other arithmetic  21.1 us (2%)
  between operations  13.8 us (1%)
    psum x1, blocking collectives, local(): key_sum, value_sum = lax.psum((key_total, value_total), 'seq')  404 us
    reduce_scatter x1, waiting for transfers between devices, local(): lax.psum_scatter(input_part, 'seq', scatter_dimension=0, tiled=True)  385 us
    psum x1, waiting for transfers between devices, local(): lax.psum(back_part.astype(jnp.bfloat16), 'heads').astype(jnp.float32)  42.7 us
    dot_general x4, matrix products, attend(): jnp.einsum('hrg,rhd->ghd', weights_low, grad_block, preferred_element_typ...  26.1 us
  transfers between devices with their start and end apart: 3, of which 3 were waited for; matrix products, arithmetic and copies ran while one was open for 0% of the time, Pallas kernels for 0%

profile of v1, /device:TPU:0, one launch (start us, length us, event | category | flops | bytes accessed | tf_op | source)
XLA Modules:
  0.0 988.0 jit_solution(10260480454568919851)
XLA Ops:
  7.2 0.0 reduce-scatter.3.cloned.1.call-start
  7.3 1.4 copy.22
  8.6 0.3 copy.25
  8.9 1.3 copy.23
  10.2 1.0 copy.27
  11.2 4.0 reshape.33
  15.2 4.0 reshape.35
  19.2 83.3 %while.15 = (s32[]{:T(128)}, f32[512,4,128]{0,2,1:T(8,128)}, f32[512,4,128]{0,2,1:T(8,128)}, bf16[4,512,4,128]{3,2,1,0:T(4,128)(2,1)}, bf16[4,512,4,128]{3,2,1,0...) while((s32[]{:T(128)}, f32[512,4,128]{0,2,1:T(8,128)}, ...), condition=%wide.region_4.5_spmd.clone, body=%wide.region_0.4_spmd.clone.sunk | while | flops 1360528384 | bytes 93372648 | solution.py:74
  19.2 2.4 constant_dynamic-slice_fusion.3
  21.5 0.7 fusion.81
  22.3 3.2 fusion.82
  25.5 6.4 fusion.84
  31.8 3.4 multiply_reduce_fusion.3
  35.2 0.4 copy-done.1
  35.6 1.2 multiply_convert_fusion.2
  36.8 0.9 fusion.83
  37.7 0.9 fusion.85
  38.6 1.2 copy_dynamic-update-slice_fusion.2
  39.9 2.4 constant_dynamic-slice_fusion.3
  42.2 0.7 fusion.81
  43.0 3.2 fusion.82
  46.1 6.6 fusion.84
  52.7 3.4 multiply_reduce_fusion.3
  56.1 0.4 copy-done.1
  56.5 1.2 multiply_convert_fusion.2
  57.7 0.9 fusion.83
  58.6 0.9 fusion.85
  59.5 1.2 copy_dynamic-update-slice_fusion.2
  60.7 2.4 constant_dynamic-slice_fusion.3
  63.1 0.7 fusion.81
  63.8 3.2 fusion.82
  67.0 6.6 fusion.84
  73.6 3.4 multiply_reduce_fusion.3
  77.0 0.4 copy-done.1
  77.3 1.2 multiply_convert_fusion.2
  78.6 0.9 fusion.83
  79.5 0.9 fusion.85
  80.4 1.2 copy_dynamic-update-slice_fusion.2
  81.6 2.4 constant_dynamic-slice_fusion.3
  84.0 0.7 fusion.81
  84.7 3.2 fusion.82
  87.9 6.6 fusion.84
  94.4 3.4 multiply_reduce_fusion.3
  97.8 0.4 copy-done.1
  98.2 1.2 multiply_convert_fusion.2
  99.4 0.9 fusion.83
  100.3 0.9 fusion.85
  101.3 1.2 copy_dynamic-update-slice_fusion.2
  102.5 2.3 broadcast_multiply_fusion
  104.8 403.7 %all-reduce.6 = (bf16[512,512]{0,1:T(8,128)(2,1)S(1)}, bf16[512,512]{0,1:T(8,128)(2,1)S(1)}) all-reduce(f32[512,512]{0,1:T(8,128)} %bitcast.71, f32[512,512]{0,1:T(8,128)} %bitcast.76), channel_id=1, replica_groups=mesh['seq'=64,'heads'=4] {'seq'}, use_global_device_ids=true, to_apply=%region_5.6 | all-reduce | flops 524288 | bytes 3145728 | tf_op jit(solution)/shard_map/psum | solution.py:80
  508.5 1.3 fusion.48
  509.8 0.3 copy-done.5
  510.1 2.6 add_convert_fusion
  512.7 0.0 all-reduce.5.cloned.1.call-start
  512.8 19.3 %all_to_all.5 = bf16[64,8,512]{2,1,0:T(8,128)(2,1)S(1)} all-to-all(bf16[64,8,512]{2,1,0:T(8,128)(2,1)S(1)} %stack.2), channel_id=1, replica_groups=mesh['seq'=64,'heads'=4] {'seq'}, dimensions={0} | all-to-all | bytes 1048576 | tf_op jit(solution)/shard_map/all_to_all | solution.py:12
  532.1 0.9 convolution_convert_fusion.1
  533.1 11.9 %reduce-scatter.3.cloned.1.call-done = bf16[512,512]{1,0:T(8,128)(2,1)} async-done(((bf16[512,2048]{1,0:T(8,128)(2,1)}), bf16[512,512]{1,0:T(8,128)(2,1)}) %reduce-scatter.3.cloned.1.call-update) | async-done | bytes 524304 | tf_op jit(solution)/shard_map/reduce_scatter | solution.py:81
  545.0 2.0 convolution_convert_fusion
  547.0 0.0 reduce-scatter.5.cloned.1.call-start
  547.0 42.7 %all-reduce.5.cloned.1.call-done = (bf16[512,128]{1,0:T(8,128)(2,1)}, bf16[512,128]{1,0:T(8,128)(2,1)}) async-done(((bf16[512,128]{1,0:T(8,128)(2,1)}, bf16[512,128]{1,0:T(8,128)(2,1)}), (bf16[512,128]{1,0:T(8,128)(2,1)}, bf16[512,128]{1,0:T(8,128)(2,1)})) %all-reduce.5.cloned.1.call-update) | async-done | bytes 262160 | tf_op jit(solution)/shard_map/psum | solution.py:95
  589.7 2.3 fusion.35
  592.0 3.3 copy.49
  595.3 384.9 %reduce-scatter.5.cloned.1.call-done = f32[8,512]{1,0:T(8,128)} async-done(((f32[512,512]{1,0:T(8,128)}), f32[8,512]{1,0:T(8,128)}) %reduce-scatter.5.cloned.1.call-update) | async-done | bytes 16400 | tf_op jit(solution)/shard_map/reduce_scatter | solution.py:99
  980.2 1.3 convert_add_fusion
  (44 shorter events, 0.3 us)
Async XLA Ops:
  7.2 501.3 %copy-start = (bf16[2048,512]{1,0:T(8,128)(2,1)S(1)}, bf16[2048,512]{1,0:T(8,128)(2,1)}, u32[]{:S(2)}) copy-start(bf16[2048,512]{1,0:T(8,128)(2,1)} %param.15) | copy-start | bytes 6291460
  7.2 537.8 %reduce-scatter.3.cloned.1.call-start = ((), (), s32[]{:S(2)}) async-start(), calls=%async_computation.3 | async-start | bytes 2621440 | tf_op jit(solution)/shard_map/reduce_scatter | solution.py:81
  22.3 3.2 copy-start.2
  31.8 3.7 copy-start.1
  35.6 1.2 copy-start.3
  37.7 2.2 copy-start.4
  42.9 3.2 copy-start.2
  52.7 3.7 copy-start.1
  56.5 1.2 copy-start.3
  58.6 2.1 copy-start.4
  63.8 3.2 copy-start.2
  73.6 3.7 copy-start.1
  77.3 1.2 copy-start.3
  79.5 2.1 copy-start.4
  84.7 3.2 copy-start.2
  94.4 3.7 copy-start.1
  98.2 1.2 copy-start.3
  100.3 2.2 copy-start.4
  508.5 1.6 copy-start.5
  510.1 2.7 copy-start.8
  510.1 22.1 %copy-start.6 = (bf16[512,128]{1,0:T(8,128)(2,1)S(1)}, bf16[512,128]{1,0:T(8,128)(2,1)}, u32[]{:S(2)}) copy-start(bf16[512,128]{1,0:T(8,128)(2,1)} %param.18) | copy-start | bytes 393220
  512.7 32.3 %copy-start.7 = (bf16[128,512]{1,0:T(8,128)(2,1)S(1)}, bf16[128,512]{1,0:T(8,128)(2,1)}, u32[]{:S(2)}) copy-start(bf16[128,512]{1,0:T(8,128)(2,1)} %param.19) | copy-start | bytes 393220
  512.7 77.0 %all-reduce.5.cloned.1.call-start = ((), (), s32[]{:S(2)}) async-start(), calls=%async_computation.5 | async-start | bytes 524288 | tf_op jit(solution)/shard_map/psum | solution.py:95
  547.0 433.2 %reduce-scatter.5.cloned.1.call-start = ((), (), s32[]{:S(2)}) async-start(), calls=%async_computation.4 | async-start | bytes 1064960 | tf_op jit(solution)/shard_map/reduce_scatter | solution.py:99
Sparse Core Ops, SparseCore 0:
  512.9 32.0 reduce-scatter.2
  548.2 41.4 all-reduce.4
  592.2 387.9 reduce-scatter.4
